TPU v7x, 32 devices: a whole 2x2x4 slice. The times are simulated.
32 devices in a mesh: pair: 4 (over x, core), blk: 8 (over z, y).
Axes of the slice: x: 2, y: 2, z: 4, core: 2. Of those that a mesh axis runs over, the one named last changes fastest.
Arguments:
- left_feats: bfloat16 [4, 64, 256, 256], P('pair', None, 'blk'), may hold values from -6 to 6
- right_feats: bfloat16 [4, 64, 256, 256], P('pair', None, 'blk'), may hold values from -6 to 6
- offsets: int32 [8], P('blk'), may hold values from 0 to 3, as said below
- hidden: bfloat16 [4, 64, 256, 128], P('pair', None, 'blk'), may hold values from -1 to 1
- context: bfloat16 [4, 3, 64, 256, 128], P('pair', None, None, 'blk'), may hold values from -6 to 6
- gru_weights: bfloat16 [2, 3, 5, 164, 128], replicated, may hold values from -0.21875 to 0.21875
- hidden_grad: float32 [4, 64, 256, 128], P('pair', None, 'blk'), may hold values from -0.06 to 0.06
Outputs:
- new_hidden: bfloat16 [4, 64, 256, 128], P('pair', None, 'blk')
- weight_grads: float32 [2, 3, 5, 164, 128], replicated
- hidden_in_grad: float32 [4, 64, 256, 128], P('pair', None, 'blk')
Inputs may be any that keep to these rules, and one draw needn't show every extreme that they name: Stripe s reads the frame-2 blocks s - offsets[s] - 1 and s - offsets[s]; some stripe has offset 4 - 1.
All inputs are finite; a program needn't handle non-finite values.
Results may differ from a plain program's by a relative error of at most 0.0054.
Values may be sent and summed in bfloat16 or wider, within the bound.
A program may use at most 128 MiB of HBM per device.

v0:
```python
import functools
import math

import jax
import jax.numpy as jnp
import numpy as np
from jax import lax
from jax.experimental import pallas as pl
from jax.experimental.pallas import tpu as pltpu
from jax.sharding import PartitionSpec as P

LEVELS = 4
RADIUS = 4


def lookup_table(column_count, level_count, radius_len):
    tap_count = 2 * radius_len + 1
    lookup = np.zeros((column_count, 2 * column_count, level_count * tap_count), np.float32)
    positions = np.arange(column_count)
    for level_id in range(level_count):
        pool_span = 2**level_id
        pooled_cols = 2 * column_count // pool_span
        for tap_id in range(tap_count):
            centre = (positions + column_count // 2) // pool_span + tap_id - radius_len
            inside = (centre >= 0) & (centre < pooled_cols)
            for inner_id in range(pool_span):
                lookup[
                    positions[inside],
                    centre[inside] * pool_span + inner_id,
                    level_id * tap_count + tap_id,
                ] = (
                    1.0 / pool_span
                )
    return lookup


MESH = pl.DeviceIdType.MESH
BAND_CHUNKS = 4


def band_kernel(count, block_ref, band_ref, send_sem, recv_sem):
    me = lax.axis_index("blk")
    odd = lax.rem(me, 2)
    mate = me + 1 - 2 * odd
    has_next = me + 2 < count
    has_prev = me >= 2
    has_far = me >= 4
    rows = block_ref.shape[0] // BAND_CHUNKS

    barrier = pltpu.get_barrier_semaphore()
    pl.semaphore_signal(barrier, inc=1, device_id={"blk": mate}, device_id_type=MESH)

    @pl.when(has_next)
    def _():
        pl.semaphore_signal(barrier, inc=1, device_id={"blk": me + 2}, device_id_type=MESH)

    @pl.when(has_prev)
    def _():
        pl.semaphore_signal(barrier, inc=1, device_id={"blk": me - 2}, device_id_type=MESH)

    pl.semaphore_wait(barrier, 1 + has_next.astype(jnp.int32) + has_prev.astype(jnp.int32))

    def copy(source, kind, slot, chunk, target):
        part = pl.ds(chunk * rows, rows)
        src = block_ref if source is None else band_ref.at[source]
        return pltpu.make_async_remote_copy(
            src_ref=src.at[part],
            dst_ref=band_ref.at[slot, part],
            send_sem=send_sem.at[kind, chunk],
            recv_sem=recv_sem.at[slot, chunk],
            device_id={"blk": target},
            device_id_type=MESH,
        )

    def onward(chunk):
        return copy(None, 0, 1, chunk, me + 2)

    def further(chunk):
        return copy(1, 1, 3, chunk, me + 2)

    chunks = range(BAND_CHUNKS)
    for c in chunks:
        pl.when(has_next)(lambda c=c: onward(c).start())
        pl.when(odd == 0)(lambda c=c: copy(None, 2, 0, c, mate).start())
    for c in chunks:

        @pl.when(has_prev)
        def _(c=c):
            onward(c).wait_recv()
            pl.when(has_next)(lambda: further(c).start())
            pl.when(odd == 0)(lambda: copy(1, 3, 2, c, mate).start())
            pl.when(odd == 1)(lambda: copy(1, 2, 0, c, mate).start())

    for c in chunks:

        @pl.when(has_far)
        def _(c=c):
            further(c).wait_recv()
            pl.when(odd == 1)(lambda: copy(3, 3, 2, c, mate).start())

    near_in = (odd == 1) | has_prev
    third_in = ((odd == 1) & has_prev) | ((odd == 0) & has_far)
    near_out = (odd == 0) | has_prev
    third_out = ((odd == 0) & has_prev) | ((odd == 1) & has_far)
    for c in chunks:
        pl.when(near_in)(lambda c=c: copy(None, 2, 0, c, mate).wait_recv())
        pl.when(third_in)(lambda c=c: copy(1, 3, 2, c, mate).wait_recv())
        pl.when(has_next)(lambda c=c: onward(c).wait_send())
        pl.when(has_next & has_prev)(lambda c=c: further(c).wait_send())
        pl.when(near_out)(lambda c=c: copy(None, 2, 0, c, mate).wait_send())
        pl.when(third_out)(lambda c=c: copy(1, 3, 2, c, mate).wait_send())


def band_exchange(block, count):
    return pl.pallas_call(
        functools.partial(band_kernel, count),
        out_shape=jax.ShapeDtypeStruct((4,) + block.shape, block.dtype),
        in_specs=[pl.BlockSpec(memory_space=pl.ANY)],
        out_specs=pl.BlockSpec(memory_space=pl.ANY),
        scratch_shapes=[
            pltpu.SemaphoreType.DMA((4, BAND_CHUNKS)),
            pltpu.SemaphoreType.DMA((4, BAND_CHUNKS)),
        ],
        compiler_params=pltpu.CompilerParams(collective_id=0, has_side_effects=True),
        name="band_exchange",
    )(block)


def sum_steps(pairs, blks):
    steps = []
    for axis, size in (("pair", pairs), ("blk", blks)):
        mask = 1
        while mask < size:
            steps.append((axis, mask))
            mask *= 2
    return steps


def sum_kernel(steps, g_ref, out_ref, acc, sbuf, rbuf, send_sem, recv_sem):
    places = {axis: lax.axis_index(axis) for axis, _ in steps}
    barrier = pltpu.get_barrier_semaphore()
    partners = []
    bits = []
    for axis, mask in steps:
        place = places[axis]
        bit = lax.rem(place // mask, 2)
        bits.append(bit)
        partners.append({axis: place + mask * (1 - 2 * bit)})
        pl.semaphore_signal(barrier, inc=1, device_id=partners[-1], device_id_type=MESH)
    pl.semaphore_wait(barrier, len(steps))
    total = g_ref.shape[0]
    start = 0
    length = total
    landed = 0
    starts = []
    source = g_ref
    for k in range(len(steps)):
        half = length // 2
        keep = pl.multiple_of(start + bits[k] * half, 16)
        away = pl.multiple_of(start + (1 - bits[k]) * half, 16)
        sbuf[pl.ds(away, half)] = source[pl.ds(away, half)].astype(jnp.bfloat16)
        copy = pltpu.make_async_remote_copy(
            src_ref=sbuf.at[pl.ds(away, half)],
            dst_ref=rbuf.at[pl.ds(landed, half)],
            send_sem=send_sem.at[0, k],
            recv_sem=recv_sem.at[0, k],
            device_id=partners[k],
            device_id_type=MESH,
        )
        copy.start()
        copy.wait()
        acc[pl.ds(keep, half)] = source[pl.ds(keep, half)] + rbuf[pl.ds(landed, half)].astype(jnp.float32)
        source = acc
        starts.append(start)
        landed += half
        start = keep
        length = half
    out_ref[pl.ds(start, length)] = acc[pl.ds(start, length)].astype(jnp.bfloat16)
    for k in reversed(range(len(steps))):
        copy = pltpu.make_async_remote_copy(
            src_ref=out_ref.at[pl.ds(start, length)],
            dst_ref=out_ref.at[pl.ds(start, length)],
            send_sem=send_sem.at[1, k],
            recv_sem=recv_sem.at[1, k],
            device_id=partners[k],
            device_id_type=MESH,
        )
        copy.start()
        copy.wait()
        start = starts[k]
        if k:
            start = pl.multiple_of(start, 16)
        length *= 2


def all_sum(rows, pairs, blks):
    steps = sum_steps(pairs, blks)
    return pl.pallas_call(
        functools.partial(sum_kernel, steps),
        out_shape=jax.ShapeDtypeStruct(rows.shape, jnp.bfloat16),
        in_specs=[pl.BlockSpec(memory_space=pltpu.VMEM)],
        out_specs=pl.BlockSpec(memory_space=pltpu.VMEM),
        scratch_shapes=[
            pltpu.VMEM(rows.shape, jnp.float32),
            pltpu.VMEM(rows.shape, jnp.bfloat16),
            pltpu.VMEM(rows.shape, jnp.bfloat16),
            pltpu.SemaphoreType.DMA((2, len(steps))),
            pltpu.SemaphoreType.DMA((2, len(steps))),
        ],
        compiler_params=pltpu.CompilerParams(
            collective_id=1, has_side_effects=True, vmem_limit_bytes=32 * 1024 * 1024
        ),
        name="all_sum",
    )(rows)


def sum_rows_count(used, devices):
    step = devices * 16
    return -(-used // step) * step


NT = (((1,), (1,)), ((), ()))


def flat(values):
    return values.reshape(-1, values.shape[-1])


def core_kernel(
    count,
    piece,
    left_ref,
    window_ref,
    table_ref,
    hidden_ref,
    context_ref,
    weights_ref,
    grad_ref,
    new_ref,
    hidden_back_ref,
    g_ref,
    corr,
    x0,
    x1,
    rx0,
    rx1,
    dq0,
    dq1,
    dzr0,
    dzr1,
    ctx0,
    z0,
    r0,
    q0,
    z1,
    r1,
    g0,
    acc,
    send_sem,
    recv_sem,
):
    height, width, hd = hidden_ref.shape
    taps = weights_ref.shape[2]
    me = lax.axis_index("blk")
    has_left = me >= 1
    has_right = me + 1 < count
    bf16, f32 = jnp.bfloat16, jnp.float32
    part = 16

    for ref in (x0, x1, rx0, rx1, dq0, dq1, dzr0, dzr1):
        edge = jnp.zeros((2,) + ref.shape[1:], bf16)
        ref[pl.ds(0, 2)] = edge
        ref[pl.ds(ref.shape[0] - 2, 2)] = edge

    barrier = pltpu.get_barrier_semaphore()

    @pl.when(has_left)
    def _():
        pl.semaphore_signal(barrier, inc=1, device_id={"blk": me - 1}, device_id_type=MESH)

    @pl.when(has_right)
    def _():
        pl.semaphore_signal(barrier, inc=1, device_id={"blk": me + 1}, device_id_type=MESH)

    pl.semaphore_wait(barrier, has_left.astype(jnp.int32) + has_right.astype(jnp.int32))

    def edges(ref, number):
        to_left = pltpu.make_async_remote_copy(
            src_ref=ref.at[pl.ds(2, 2)],
            dst_ref=ref.at[pl.ds(width + 2, 2)],
            send_sem=send_sem.at[number, 0],
            recv_sem=recv_sem.at[number, 0],
            device_id={"blk": me - 1},
            device_id_type=MESH,
        )
        to_right = pltpu.make_async_remote_copy(
            src_ref=ref.at[pl.ds(width, 2)],
            dst_ref=ref.at[pl.ds(0, 2)],
            send_sem=send_sem.at[number, 1],
            recv_sem=recv_sem.at[number, 1],
            device_id={"blk": me + 1},
            device_id_type=MESH,
        )
        return to_left, to_right

    def send_edges(ref, number):
        to_left, to_right = edges(ref, number)
        pl.when(has_left)(lambda: to_left.start())
        pl.when(has_right)(lambda: to_right.start())

    def wait_edges(ref, number):
        to_left, to_right = edges(ref, number)
        pl.when(has_left)(lambda: to_left.wait_send())
        pl.when(has_right)(lambda: to_right.wait_send())
        pl.when(has_right)(lambda: to_left.wait_recv())
        pl.when(has_left)(lambda: to_right.wait_recv())

    @pl.loop(0, height // part)
    def _(c):
        rows = pl.ds(pl.multiple_of(c * part, part), part)
        x0[pl.ds(2, width), rows, pl.ds(0, hd)] = jnp.swapaxes(
            hidden_ref[rows].astype(f32), 0, 1
        ).astype(bf16)
        for gate in range(3):
            ctx0[gate, :, rows] = jnp.swapaxes(context_ref[gate, rows].astype(f32), 0, 1)
        scores = jnp.einsum("hxc,hjc->hxj", left_ref[rows], window_ref[rows], preferred_element_type=f32)
        scores = jnp.swapaxes(scores, 0, 1)
        high = scores.astype(bf16).astype(f32)
        corr[:, rows] = jnp.concatenate([high, scores - high], axis=-1)

    @pl.loop(0, width // part)
    def _(c):
        cols = pl.ds(pl.multiple_of(c * part, part), part)
        feats = jnp.einsum(
            "xhj,xjf->xhf", corr[cols].astype(bf16), table_ref[cols], preferred_element_type=f32
        )
        x0[pl.ds(2 + c * part, part), :, pl.ds(hd, hd)] = feats.astype(bf16)
        x1[pl.ds(2, height), cols, pl.ds(hd, hd)] = jnp.swapaxes(feats, 0, 1).astype(bf16)

    send_edges(x0, 0)
    wait_edges(x0, 0)

    def gates(section, x, rx, z, r, context, c):
        total = None
        for k in range(taps):
            w = jnp.concatenate([weights_ref[section, 0, k], weights_ref[section, 1, k]], axis=1)
            term = jnp.dot(flat(x[pl.ds(c * part + k, part)]), w, preferred_element_type=f32)
            total = term if total is None else total + term
        shape = (part,) + x.shape[1:2] + (hd,)
        here = pl.ds(c * part, part)
        z[here] = jax.nn.sigmoid(total[:, :hd].reshape(shape) + context(0, here))
        reset = jax.nn.sigmoid(total[:, hd:].reshape(shape) + context(1, here))
        r[here] = reset
        own = x[pl.ds(c * part + 2, part), :, pl.ds(0, hd)].astype(f32)
        rx[pl.ds(c * part + 2, part)] = (reset * own).astype(bf16)

    def gated(x, rx, first):
        there = pl.ds(first, part)
        return jnp.concatenate([flat(rx[there]), flat(x[there, :, pl.ds(hd, hd)])], axis=1)

    def candidate(section, x, rx, context, c):
        total = None
        for k in range(taps):
            term = jnp.dot(
                gated(x, rx, c * part + k), weights_ref[section, 2, k], preferred_element_type=f32
            )
            total = term if total is None else total + term
        shape = (part,) + x.shape[1:2] + (hd,)
        return jnp.tanh(total.reshape(shape) + context(2, pl.ds(c * part, part)))

    def context_h(gate, here):
        return ctx0[gate, here]

    def context_v(gate, here):
        return context_ref[gate, here].astype(f32)

    @pl.loop(0, width // part)
    def _(c):
        gates(0, x0, rx0, z0, r0, context_h, c)

    send_edges(rx0, 1)
    wait_edges(rx0, 1)

    @pl.loop(0, width // part)
    def _(c):
        here = pl.ds(c * part, part)
        q = candidate(0, x0, rx0, context_h, c)
        q0[here] = q
        z = z0[here]
        own = x0[pl.ds(c * part + 2, part), :, pl.ds(0, hd)].astype(f32)
        blended = (1.0 - z) * own + z * q
        cols = pl.ds(pl.multiple_of(c * part, part), part)
        x1[pl.ds(2, height), cols, pl.ds(0, hd)] = jnp.swapaxes(blended, 0, 1).astype(bf16)

    @pl.loop(0, height // part)
    def _(c):
        gates(1, x1, rx1, z1, r1, context_v, c)

    def deltas(g, z, q, own, dq, dzr, inner):
        dq[inner] = (g * z * (1.0 - q * q)).astype(bf16)
        dzr[inner, :, pl.ds(0, hd)] = (g * (q - own) * z * (1.0 - z)).astype(bf16)

    @pl.loop(0, height // part)
    def _(c):
        here = pl.ds(c * part, part)
        inner = pl.ds(c * part + 2, part)
        q = candidate(1, x1, rx1, context_v, c)
        z = z1[here]
        own = x1[inner, :, pl.ds(0, hd)].astype(f32)
        new_ref[here] = ((1.0 - z) * own + z * q).astype(bf16)
        deltas(grad_ref[here], z, q, own, dq1, dzr1, inner)

    def back_reset(section, x, g, z, r, dq, dzr, c):
        here = pl.ds(c * part, part)
        inner = pl.ds(c * part + 2, part)
        total = None
        for k in range(taps):
            term = lax.dot_general(
                flat(dq[pl.ds(c * part + taps - 1 - k, part)]),
                weights_ref[section, 2, k, pl.ds(0, hd)],
                NT,
                preferred_element_type=f32,
            )
            total = term if total is None else total + term
        total = total.reshape((part,) + x.shape[1:2] + (hd,))
        reset = r[here]
        own = x[inner, :, pl.ds(0, hd)].astype(f32)
        dzr[inner, :, pl.ds(hd, hd)] = (total * own * reset * (1.0 - reset)).astype(bf16)
        r[here] = g[here] * (1.0 - z[here]) + total * reset

    def back_hidden(section, r, dzr, c):
        total = None
        for k in range(taps):
            w = jnp.concatenate(
                [
                    weights_ref[section, 0, k, pl.ds(0, hd)],
                    weights_ref[section, 1, k, pl.ds(0, hd)],
                ],
                axis=1,
            )
            term = lax.dot_general(
                flat(dzr[pl.ds(c * part + taps - 1 - k, part)]), w, NT, preferred_element_type=f32
            )
            total = term if total is None else total + term
        total = total.reshape((part,) + dzr.shape[1:2] + (hd,))
        return r[pl.ds(c * part, part)] + total

    def weight_grads_zr(section, x, dzr, blocks):
        acc[...] = jnp.zeros_like(acc)

        @pl.loop(0, blocks)
        def _(c):
            d = flat(dzr[pl.ds(c * part + 2, part)]).astype(f32).T.astype(bf16)
            for k in range(taps):
                acc[k] += jnp.dot(d, flat(x[pl.ds(c * part + k, part)]), preferred_element_type=f32)

        for k in range(taps):
            for gate in range(2):
                place = ((section * 3 + gate) * taps + k) * piece
                g_ref[pl.ds(place, piece)] = acc[k, pl.ds(gate * hd, hd)].T[:piece]

    def weight_grads_q(section, x, rx, dq, blocks):
        half = pl.ds(0, hd)
        acc[:, half] = jnp.zeros((taps, hd, 2 * hd), f32)

        @pl.loop(0, blocks)
        def _(c):
            d = flat(dq[pl.ds(c * part + 2, part)]).astype(f32).T.astype(bf16)
            for k in range(taps):
                acc[k, half] += jnp.dot(d, gated(x, rx, c * part + k), preferred_element_type=f32)

        for k in range(taps):
            place = ((section * 3 + 2) * taps + k) * piece
            g_ref[pl.ds(place, piece)] = acc[k, half].T[:piece]

    @pl.loop(0, height // part)
    def _(c):
        back_reset(1, x1, grad_ref, z1, r1, dq1, dzr1, c)

    @pl.loop(0, height // part)
    def _(c):
        rows = pl.ds(pl.multiple_of(c * part, part), part)
        g0[:, rows] = jnp.swapaxes(back_hidden(1, r1, dzr1, c), 0, 1)

    @pl.loop(0, width // part)
    def _(c):
        here = pl.ds(c * part, part)
        inner = pl.ds(c * part + 2, part)
        own = x0[inner, :, pl.ds(0, hd)].astype(f32)
        deltas(g0[here], z0[here], q0[here], own, dq0, dzr0, inner)

    send_edges(dq0, 2)
    weight_grads_zr(1, x1, dzr1, height // part)
    weight_grads_q(1, x1, rx1, dq1, height // part)
    wait_edges(dq0, 2)

    @pl.loop(0, width // part)
    def _(c):
        back_reset(0, x0, g0, z0, r0, dq0, dzr0, c)

    send_edges(dzr0, 3)
    weight_grads_q(0, x0, rx0, dq0, width // part)
    weight_grads_zr(0, x0, dzr0, width // part)
    wait_edges(dzr0, 3)

    @pl.loop(0, width // part)
    def _(c):
        cols = pl.ds(pl.multiple_of(c * part, part), part)
        hidden_back_ref[:, cols] = jnp.swapaxes(back_hidden(0, r0, dzr0, c), 0, 1)

    used = 2 * 3 * taps * piece
    if used < g_ref.shape[0]:
        g_ref[pl.ds(used, g_ref.shape[0] - used)] = jnp.zeros((g_ref.shape[0] - used, hd), f32)


def core(left, window, table, hidden, context, weights, hidden_grad, count, piece, sum_rows):
    height, width, hd = hidden.shape
    taps = weights.shape[2]
    bf16, f32 = jnp.bfloat16, jnp.float32
    vmem = pl.BlockSpec(memory_space=pltpu.VMEM)
    across = (width, height, hd)
    down = (height, width, hd)

    def padded(shape, wide):
        return pltpu.VMEM((shape[0] + 4, shape[1], wide * hd), bf16)

    return pl.pallas_call(
        functools.partial(core_kernel, count, piece),
        out_shape=(
            jax.ShapeDtypeStruct(hidden.shape, bf16),
            jax.ShapeDtypeStruct(hidden.shape, f32),
            jax.ShapeDtypeStruct((sum_rows, hd), f32),
        ),
        in_specs=[vmem] * 7,
        out_specs=(vmem,) * 3,
        scratch_shapes=[
            pltpu.VMEM((width, height, 4 * width), f32),
            padded(across, 2),
            padded(down, 2),
            padded(across, 1),
            padded(down, 1),
            padded(across, 1),
            padded(down, 1),
            padded(across, 2),
            padded(down, 2),
            pltpu.VMEM((3,) + across, f32),
            pltpu.VMEM(across, f32),
            pltpu.VMEM(across, f32),
            pltpu.VMEM(across, f32),
            pltpu.VMEM(down, f32),
            pltpu.VMEM(down, f32),
            pltpu.VMEM(across, f32),
            pltpu.VMEM((taps, 2 * hd, 2 * hd), f32),
            pltpu.SemaphoreType.DMA((4, 2)),
            pltpu.SemaphoreType.DMA((4, 2)),
        ],
        compiler_params=pltpu.CompilerParams(
            collective_id=2, has_side_effects=True, vmem_limit_bytes=58 * 1024 * 1024
        ),
        name="core",
    )(left, window, table, hidden, context, weights, hidden_grad)


def on_device(left_feats, right_feats, offsets, hidden, context, gru_weights, hidden_grad):
    left_block = left_feats[0]
    right_block = right_feats[0]
    offset = offsets[0]
    stripe = lax.axis_index("blk")
    column_count = left_block.shape[1]
    empty_block = jnp.zeros_like(right_block)
    low_id = stripe - offset - 1
    high_id = stripe - offset
    band = band_exchange(right_block, lax.axis_size("blk"))

    def pick_one(block_id):
        distance = jnp.clip(stripe - block_id, 0, 4)
        picked = lax.dynamic_index_in_dim(band, jnp.maximum(distance - 1, 0), 0, keepdims=False)
        picked = jnp.where(distance == 0, right_block, picked)
        return jnp.where(block_id >= 0, picked, empty_block)

    low_block = pick_one(low_id)
    high_block = pick_one(high_id)
    window = jnp.concatenate([low_block, high_block], axis=1)
    table = lookup_table(column_count, LEVELS, RADIUS) / math.sqrt(left_block.shape[-1])
    hd = gru_weights.shape[-1]
    table = np.concatenate([table, table], axis=1)
    table = np.pad(table, ((0, 0), (0, 0), (0, hd - table.shape[2])))
    table = jnp.asarray(table, jnp.bfloat16)
    pairs, blks = lax.axis_size("pair"), lax.axis_size("blk")
    shape = gru_weights.shape
    piece = -(-shape[3] // 8) * 8
    used = math.prod(shape[:3]) * piece
    weights = jnp.pad(gru_weights, ((0, 0),) * 3 + ((0, 2 * hd - shape[3]), (0, 0)))
    new_hidden, hidden_back, rows = core(
        left_block,
        window,
        table,
        hidden[0],
        context[0],
        weights,
        hidden_grad[0],
        blks,
        piece,
        sum_rows_count(used, pairs * blks),
    )
    summed = all_sum(rows, pairs, blks)[:used].reshape(shape[:3] + (piece, hd))
    grad_stack = summed[:, :, :, : shape[3]].astype(jnp.float32)
    return (new_hidden[None], grad_stack, hidden_back[None])


def solution(mesh):
    placed = (
        P("pair", None, "blk", None),
        P("pair", None, "blk", None),
        P("blk"),
        P("pair", None, "blk", None),
        P("pair", None, None, "blk", None),
        P(),
        P("pair", None, "blk", None),
    )
    return jax.shard_map(
        on_device,
        mesh=mesh,
        in_specs=placed,
        out_specs=(P("pair", None, "blk", None), P(), P("pair", None, "blk", None)),
        check_vma=False,
    )
```

profile of v0, /device:TPU:0, one launch (start us, length us, event | category | flops | bytes accessed | tf_op | source)
XLA Modules:
  0.0 157.7 jit_solution(6984891637903427056)
XLA Ops:
  1.3 0.0 copy-start.1
  1.3 26.1 %band_exchange.1 = bf16[4,64,32,256]{3,2,1,0:T(8,128)(2,1)} custom-call(bf16[64,32,256]{2,1,0:T(8,128)(2,1)} %bitcast.23), custom_call_target="tpu_custom_call" | custom-call | tf_op jit(solution)/shard_map/band_exchange/pallas_call | solution.py:115
  27.5 0.0 copy-done.1
  27.5 1.7 %fusion.1 = (bf16[64,32,256]{2,1,0:T(8,128)(2,1)S(1)}, bf16[64,32,256]{2,1,0:T(8,128)(2,1)S(1)}) fusion(bf16[4,64,32,256]{3,2,1,0:T(8,128)(2,1)} %band_exchange.1, s32[]{:T(128)S(6)} %max.14, pred[]{:T(512)S(6)} %eq.6, pred[]{:T(512)S(6)} %ge.6, bf16[1,64,32,256]{3,2,1,0:T(8,128)(2,1)S(1)} %copy-done.1, s32[]{:T(128)S(6)} %max.16, pred[]{:T(512)S(6)} %eq.7, ...), kind=kLoop, calls=%fused_computation.5 | loop fusion | flops 2097152 | bytes 5242892 | tf_op jit(solution)/shard_map/jit(_where)/select_n | solution.py:579
  29.2 0.0 copy-start.2
  29.2 1.5 pad_maximum_fusion.window_ref
  30.7 0.2 copy-done.2
  30.9 0.2 copy.11
  31.1 1.6 pad.4.weights_ref
  32.6 70.9 %core.1 = (bf16[64,32,128]{2,1,0:T(8,128)(2,1)}, f32[64,32,128]{2,1,0:T(8,128)}, f32[5120,128]{1,0:T(8,128)}) custom-call(bf16[64,32,256]{2,1,0:T(8,128)(2,1)} %bitcast.25, bf16[64,64,256]{2,1,0:T(8,128)(2,1)} %pad_maximum_fusion.window_ref, bf16[32,128,128]{2,1,0:T(8,128)(2,1)} %constant.26.clone.table_ref, bf16[64,32,128]{2,1,0:T(8,128)(2,1)} %bitcast.28, ...), custom_call_target="tpu_custom_call" | custom-call | tf_op jit(solution)/shard_map/core/pallas_call | solution.py:527
  103.6 0.0 copy-start
  103.6 1.7 %copy-done = f32[5120,128]{1,0:T(8,128)S(1)} copy-done((f32[5120,128]{1,0:T(8,128)S(1)}, f32[5120,128]{1,0:T(8,128)}, u32[]{:S(2)}) %copy-start) | copy-done | bytes 2621464
  105.3 48.1 %all_sum.1 = bf16[5120,128]{1,0:T(8,128)(2,1)S(1)} custom-call(f32[5120,128]{1,0:T(8,128)S(1)} %copy-done), custom_call_target="tpu_custom_call" | custom-call | tf_op jit(solution)/shard_map/all_sum/pallas_call | solution.py:198
  153.4 0.1 slice.6
  153.5 0.0 copy-start.4
  153.5 0.0 copy-start.3
  153.5 2.4 %copy_convert_fusion = f32[2,3,5,164,128]{4,0,3,2,1:T(2,128)} fusion(bf16[2,3,5,164,128]{4,3,2,1,0:T(8,128)(2,1)S(1)} %bitcast.22), kind=kLoop, calls=%fused_computation.1 | loop fusion | flops 629760 | bytes 3778560 | tf_op jit(solution)/shard_map/convert_element_type | solution.py:607
  155.9 0.0 copy-done.4
  155.9 0.8 copy.18
  156.7 0.0 copy-done.3
  156.7 1.0 copy.19
Async XLA Ops:
  1.3 26.2 %copy-start.1 = (bf16[1,64,32,256]{3,2,1,0:T(8,128)(2,1)S(1)}, bf16[1,64,32,256]{3,2,1,0:T(8,128)(2,1)}, u32[]{:S(2)}) copy-start(bf16[1,64,32,256]{3,2,1,0:T(8,128)(2,1)} %param.9) | copy-start | bytes 3145732
  29.2 1.7 %copy-start.2 = (bf16[2,3,5,164,128]{4,0,3,2,1:T(2,128)(2,1)S(1)}, bf16[2,3,5,164,128]{4,0,3,2,1:T(2,128)(2,1)}, u32[]{:S(2)}) copy-start(bf16[2,3,5,164,128]{4,0,3,2,1:T(2,128)(2,1)} %param.13) | copy-start | bytes 3778564
  103.6 1.7 %copy-start = (f32[5120,128]{1,0:T(8,128)S(1)}, f32[5120,128]{1,0:T(8,128)}, u32[]{:S(2)}) copy-start(f32[5120,128]{1,0:T(8,128)} %get-tuple-element.7.g_ref) | copy-start | bytes 7864324
  153.5 2.5 %copy-start.4 = (bf16[64,32,128]{2,1,0:T(8,128)(2,1)S(1)}, bf16[64,32,128]{2,1,0:T(8,128)(2,1)}, u32[]{:S(2)}) copy-start(bf16[64,32,128]{2,1,0:T(8,128)(2,1)} %get-tuple-element.6) | copy-start | bytes 1572868
  153.5 3.2 %copy-start.3 = (f32[64,32,128]{2,1,0:T(8,128)S(1)}, f32[64,32,128]{2,1,0:T(8,128)}, u32[]{:S(2)}) copy-start(f32[64,32,128]{2,1,0:T(8,128)} %get-tuple-element.8) | copy-start | bytes 3145732
where the time goes:
time: 158 us
  Pallas kernels  145 us (92%)
  other arithmetic  5.66 us (4%)
  local copies, waits for them, and re-layouts  5.52 us (3%)
    pallas_call x1, Pallas kernels, core(): pl.pallas_call(functools.partial(core_kernel, count, piece), out_shape=(j...  70.9 us
    pallas_call x1, Pallas kernels, all_sum(): pl.pallas_call(functools.partial(sum_kernel, steps), out_shape=jax.ShapeD...  48.1 us
    pallas_call x1, Pallas kernels, band_exchange(): pl.pallas_call(functools.partial(band_kernel, count), out_shape=jax.Shape...  26.1 us
    unnamed x13, local copies, waits for them, and re-layouts  3.87 us

commit v1 on v0

--- a/solution.py
+++ b/solution.py
@@ -35,95 +35,7 @@
 
 
 MESH = pl.DeviceIdType.MESH
-BAND_CHUNKS = 4
-
-
-def band_kernel(count, block_ref, band_ref, send_sem, recv_sem):
-    me = lax.axis_index("blk")
-    odd = lax.rem(me, 2)
-    mate = me + 1 - 2 * odd
-    has_next = me + 2 < count
-    has_prev = me >= 2
-    has_far = me >= 4
-    rows = block_ref.shape[0] // BAND_CHUNKS
-
-    barrier = pltpu.get_barrier_semaphore()
-    pl.semaphore_signal(barrier, inc=1, device_id={"blk": mate}, device_id_type=MESH)
-
-    @pl.when(has_next)
-    def _():
-        pl.semaphore_signal(barrier, inc=1, device_id={"blk": me + 2}, device_id_type=MESH)
-
-    @pl.when(has_prev)
-    def _():
-        pl.semaphore_signal(barrier, inc=1, device_id={"blk": me - 2}, device_id_type=MESH)
-
-    pl.semaphore_wait(barrier, 1 + has_next.astype(jnp.int32) + has_prev.astype(jnp.int32))
-
-    def copy(source, kind, slot, chunk, target):
-        part = pl.ds(chunk * rows, rows)
-        src = block_ref if source is None else band_ref.at[source]
-        return pltpu.make_async_remote_copy(
-            src_ref=src.at[part],
-            dst_ref=band_ref.at[slot, part],
-            send_sem=send_sem.at[kind, chunk],
-            recv_sem=recv_sem.at[slot, chunk],
-            device_id={"blk": target},
-            device_id_type=MESH,
-        )
-
-    def onward(chunk):
-        return copy(None, 0, 1, chunk, me + 2)
-
-    def further(chunk):
-        return copy(1, 1, 3, chunk, me + 2)
-
-    chunks = range(BAND_CHUNKS)
-    for c in chunks:
-        pl.when(has_next)(lambda c=c: onward(c).start())
-        pl.when(odd == 0)(lambda c=c: copy(None, 2, 0, c, mate).start())
-    for c in chunks:
-
-        @pl.when(has_prev)
-        def _(c=c):
-            onward(c).wait_recv()
-            pl.when(has_next)(lambda: further(c).start())
-            pl.when(odd == 0)(lambda: copy(1, 3, 2, c, mate).start())
-            pl.when(odd == 1)(lambda: copy(1, 2, 0, c, mate).start())
-
-    for c in chunks:
-
-        @pl.when(has_far)
-        def _(c=c):
-            further(c).wait_recv()
-            pl.when(odd == 1)(lambda: copy(3, 3, 2, c, mate).start())
-
-    near_in = (odd == 1) | has_prev
-    third_in = ((odd == 1) & has_prev) | ((odd == 0) & has_far)
-    near_out = (odd == 0) | has_prev
-    third_out = ((odd == 0) & has_prev) | ((odd == 1) & has_far)
-    for c in chunks:
-        pl.when(near_in)(lambda c=c: copy(None, 2, 0, c, mate).wait_recv())
-        pl.when(third_in)(lambda c=c: copy(1, 3, 2, c, mate).wait_recv())
-        pl.when(has_next)(lambda c=c: onward(c).wait_send())
-        pl.when(has_next & has_prev)(lambda c=c: further(c).wait_send())
-        pl.when(near_out)(lambda c=c: copy(None, 2, 0, c, mate).wait_send())
-        pl.when(third_out)(lambda c=c: copy(1, 3, 2, c, mate).wait_send())
-
-
-def band_exchange(block, count):
-    return pl.pallas_call(
-        functools.partial(band_kernel, count),
-        out_shape=jax.ShapeDtypeStruct((4,) + block.shape, block.dtype),
-        in_specs=[pl.BlockSpec(memory_space=pl.ANY)],
-        out_specs=pl.BlockSpec(memory_space=pl.ANY),
-        scratch_shapes=[
-            pltpu.SemaphoreType.DMA((4, BAND_CHUNKS)),
-            pltpu.SemaphoreType.DMA((4, BAND_CHUNKS)),
-        ],
-        compiler_params=pltpu.CompilerParams(collective_id=0, has_side_effects=True),
-        name="band_exchange",
-    )(block)
+BAND_CHUNKS = 8
 
 
 def sum_steps(pairs, blks):
@@ -136,84 +48,6 @@
     return steps
 
 
-def sum_kernel(steps, g_ref, out_ref, acc, sbuf, rbuf, send_sem, recv_sem):
-    places = {axis: lax.axis_index(axis) for axis, _ in steps}
-    barrier = pltpu.get_barrier_semaphore()
-    partners = []
-    bits = []
-    for axis, mask in steps:
-        place = places[axis]
-        bit = lax.rem(place // mask, 2)
-        bits.append(bit)
-        partners.append({axis: place + mask * (1 - 2 * bit)})
-        pl.semaphore_signal(barrier, inc=1, device_id=partners[-1], device_id_type=MESH)
-    pl.semaphore_wait(barrier, len(steps))
-    total = g_ref.shape[0]
-    start = 0
-    length = total
-    landed = 0
-    starts = []
-    source = g_ref
-    for k in range(len(steps)):
-        half = length // 2
-        keep = pl.multiple_of(start + bits[k] * half, 16)
-        away = pl.multiple_of(start + (1 - bits[k]) * half, 16)
-        sbuf[pl.ds(away, half)] = source[pl.ds(away, half)].astype(jnp.bfloat16)
-        copy = pltpu.make_async_remote_copy(
-            src_ref=sbuf.at[pl.ds(away, half)],
-            dst_ref=rbuf.at[pl.ds(landed, half)],
-            send_sem=send_sem.at[0, k],
-            recv_sem=recv_sem.at[0, k],
-            device_id=partners[k],
-            device_id_type=MESH,
-        )
-        copy.start()
-        copy.wait()
-        acc[pl.ds(keep, half)] = source[pl.ds(keep, half)] + rbuf[pl.ds(landed, half)].astype(jnp.float32)
-        source = acc
-        starts.append(start)
-        landed += half
-        start = keep
-        length = half
-    out_ref[pl.ds(start, length)] = acc[pl.ds(start, length)].astype(jnp.bfloat16)
-    for k in reversed(range(len(steps))):
-        copy = pltpu.make_async_remote_copy(
-            src_ref=out_ref.at[pl.ds(start, length)],
-            dst_ref=out_ref.at[pl.ds(start, length)],
-            send_sem=send_sem.at[1, k],
-            recv_sem=recv_sem.at[1, k],
-            device_id=partners[k],
-            device_id_type=MESH,
-        )
-        copy.start()
-        copy.wait()
-        start = starts[k]
-        if k:
-            start = pl.multiple_of(start, 16)
-        length *= 2
-
-
-def all_sum(rows, pairs, blks):
-    steps = sum_steps(pairs, blks)
-    return pl.pallas_call(
-        functools.partial(sum_kernel, steps),
-        out_shape=jax.ShapeDtypeStruct(rows.shape, jnp.bfloat16),
-        in_specs=[pl.BlockSpec(memory_space=pltpu.VMEM)],
-        out_specs=pl.BlockSpec(memory_space=pltpu.VMEM),
-        scratch_shapes=[
-            pltpu.VMEM(rows.shape, jnp.float32),
-            pltpu.VMEM(rows.shape, jnp.bfloat16),
-            pltpu.VMEM(rows.shape, jnp.bfloat16),
-            pltpu.SemaphoreType.DMA((2, len(steps))),
-            pltpu.SemaphoreType.DMA((2, len(steps))),
-        ],
-        compiler_params=pltpu.CompilerParams(
-            collective_id=1, has_side_effects=True, vmem_limit_bytes=32 * 1024 * 1024
-        ),
-        name="all_sum",
-    )(rows)
-
-
 def sum_rows_count(used, devices):
     step = devices * 16
     return -(-used // step) * step
@@ -229,16 +63,29 @@
 def core_kernel(
     count,
     piece,
+    steps,
+    offset_ref,
+    block_in,
+    left_in,
+    table_in,
+    hidden_in,
+    context_in,
+    weights_in,
+    grad_in,
+    new_ref,
+    hidden_back_ref,
+    sum_ref,
+    band,
     left_ref,
-    window_ref,
     table_ref,
     hidden_ref,
     context_ref,
+    narrow_ref,
+    grad_ref,
     weights_ref,
-    grad_ref,
-    new_ref,
-    hidden_back_ref,
     g_ref,
+    sbuf,
+    rbuf,
     corr,
     x0,
     x1,
@@ -258,6 +105,11 @@
     acc,
     send_sem,
     recv_sem,
+    band_send,
+    band_recv,
+    sum_send,
+    sum_recv,
+    local_sem,
 ):
     height, width, hd = hidden_ref.shape
     taps = weights_ref.shape[2]
@@ -272,17 +124,77 @@
         ref[pl.ds(0, 2)] = edge
         ref[pl.ds(ref.shape[0] - 2, 2)] = edge
 
+    for distance in range(1, 5):
+
+        @pl.when(me < distance)
+        def _(distance=distance):
+            band[distance] = jnp.zeros(band.shape[1:], bf16)
+
     barrier = pltpu.get_barrier_semaphore()
-
-    @pl.when(has_left)
-    def _():
-        pl.semaphore_signal(barrier, inc=1, device_id={"blk": me - 1}, device_id_type=MESH)
-
-    @pl.when(has_right)
-    def _():
-        pl.semaphore_signal(barrier, inc=1, device_id={"blk": me + 1}, device_id_type=MESH)
-
-    pl.semaphore_wait(barrier, has_left.astype(jnp.int32) + has_right.astype(jnp.int32))
+    places = {"pair": lax.axis_index("pair"), "blk": me}
+    bits = []
+    partners = []
+    for axis, mask in steps:
+        bit = lax.rem(places[axis] // mask, 2)
+        bits.append(bit)
+        partners.append({axis: places[axis] + mask * (1 - 2 * bit)})
+        pl.semaphore_signal(barrier, inc=1, device_id=partners[-1], device_id_type=MESH)
+    has_next = me + 2 < count
+    has_prev = me >= 2
+    has_far = me >= 4
+    expected = len(steps)
+    for present, shift in ((has_left, -1), (has_right, 1), (has_prev, -2), (has_next, 2)):
+
+        @pl.when(present)
+        def _(shift=shift):
+            pl.semaphore_signal(barrier, inc=1, device_id={"blk": me + shift}, device_id_type=MESH)
+
+        expected = expected + present.astype(jnp.int32)
+    pl.semaphore_wait(barrier, expected)
+
+    odd = lax.rem(me, 2)
+    mate = me + 1 - 2 * odd
+    band_rows = height // BAND_CHUNKS
+
+    def band_copy(source, kind, slot, chunk, target):
+        part = pl.ds(chunk * band_rows, band_rows)
+        src = block_in.at[part] if source is None else band.at[source, part]
+        return pltpu.make_async_remote_copy(
+            src_ref=src,
+            dst_ref=band.at[slot, part],
+            send_sem=band_send.at[kind, chunk],
+            recv_sem=band_recv.at[slot - 1, chunk],
+            device_id={"blk": target},
+            device_id_type=MESH,
+        )
+
+    def onward(chunk):
+        return band_copy(None, 0, 2, chunk, me + 2)
+
+    def further(chunk):
+        return band_copy(2, 1, 4, chunk, me + 2)
+
+    chunks = range(BAND_CHUNKS)
+    for c in chunks:
+        pl.when(has_next)(lambda c=c: onward(c).start())
+        pl.when(odd == 0)(lambda c=c: band_copy(None, 2, 1, c, mate).start())
+
+    local = [
+        pltpu.make_async_copy(src, dst, local_sem.at[i])
+        for i, (src, dst) in enumerate(
+            (
+                (hidden_in, hidden_ref),
+                (context_in, context_ref),
+                (weights_in, narrow_ref),
+                (left_in, left_ref),
+                (block_in, band.at[0]),
+                (table_in, table_ref),
+                (grad_in, grad_ref),
+            )
+        )
+    ]
+    for copy in local:
+        copy.start()
 
     def edges(ref, number):
         to_left = pltpu.make_async_remote_copy(
@@ -315,15 +227,65 @@
         pl.when(has_right)(lambda: to_left.wait_recv())
         pl.when(has_left)(lambda: to_right.wait_recv())
 
+    for copy in local:
+        copy.wait()
+
     @pl.loop(0, height // part)
     def _(c):
         rows = pl.ds(pl.multiple_of(c * part, part), part)
         x0[pl.ds(2, width), rows, pl.ds(0, hd)] = jnp.swapaxes(
             hidden_ref[rows].astype(f32), 0, 1
         ).astype(bf16)
+
+    for c in chunks:
+
+        @pl.when(has_prev)
+        def _(c=c):
+            onward(c).wait_recv()
+            pl.when(has_next)(lambda: further(c).start())
+            pl.when(odd == 0)(lambda: band_copy(2, 3, 3, c, mate).start())
+            pl.when(odd == 1)(lambda: band_copy(2, 2, 1, c, mate).start())
+
+    @pl.loop(0, height // part)
+    def _(c):
+        rows = pl.ds(pl.multiple_of(c * part, part), part)
         for gate in range(3):
             ctx0[gate, :, rows] = jnp.swapaxes(context_ref[gate, rows].astype(f32), 0, 1)
-        scores = jnp.einsum("hxc,hjc->hxj", left_ref[rows], window_ref[rows], preferred_element_type=f32)
+
+    deep = narrow_ref.shape[3]
+    tail = deep // 16 * 16
+    for section in range(2):
+        for gate in range(3):
+            for k in range(taps):
+                weights_ref[section, gate, k, pl.ds(0, tail)] = narrow_ref[section, gate, k, pl.ds(0, tail)]
+                rest = narrow_ref[section, gate, k, pl.ds(tail, deep - tail)].astype(f32)
+                blank = jnp.zeros((2 * hd - deep, hd), f32)
+                weights_ref[section, gate, k, pl.ds(tail, 2 * hd - tail)] = jnp.concatenate(
+                    [rest, blank], axis=0
+                ).astype(bf16)
+
+    for c in chunks:
+
+        @pl.when(has_far)
+        def _(c=c):
+            further(c).wait_recv()
+            pl.when(odd == 1)(lambda: band_copy(4, 3, 3, c, mate).start())
+
+    near_in = (odd == 1) | has_prev
+    third_in = ((odd == 1) & has_prev) | ((odd == 0) & has_far)
+    near_out = (odd == 0) | has_prev
+    third_out = ((odd == 0) & has_prev) | ((odd == 1) & has_far)
+    for c in chunks:
+        pl.when(near_in)(lambda c=c: band_copy(None, 2, 1, c, mate).wait_recv())
+        pl.when(third_in)(lambda c=c: band_copy(2, 3, 3, c, mate).wait_recv())
+
+    offset = offset_ref[0]
+
+    @pl.loop(0, height // part)
+    def _(c):
+        rows = pl.ds(pl.multiple_of(c * part, part), part)
+        window = jnp.concatenate([band[offset + 1, rows], band[offset, rows]], axis=1)
+        scores = jnp.einsum("hxc,hjc->hxj", left_ref[rows], window, preferred_element_type=f32)
         scores = jnp.swapaxes(scores, 0, 1)
         high = scores.astype(bf16).astype(f32)
         corr[:, rows] = jnp.concatenate([high, scores - high], axis=-1)
@@ -456,8 +418,8 @@
 
         for k in range(taps):
             for gate in range(2):
-                place = ((section * 3 + gate) * taps + k) * piece
-                g_ref[pl.ds(place, piece)] = acc[k, pl.ds(gate * hd, hd)].T[:piece]
+                place = (gate * taps + k) * piece
+                g_ref[section, pl.ds(place, piece)] = acc[k, pl.ds(gate * hd, hd)].T[:piece]
 
     def weight_grads_q(section, x, rx, dq, blocks):
         half = pl.ds(0, hd)
@@ -470,8 +432,8 @@
                 acc[k, half] += jnp.dot(d, gated(x, rx, c * part + k), preferred_element_type=f32)
 
         for k in range(taps):
-            place = ((section * 3 + 2) * taps + k) * piece
-            g_ref[pl.ds(place, piece)] = acc[k, half].T[:piece]
+            place = (2 * taps + k) * piece
+            g_ref[section, pl.ds(place, piece)] = acc[k, half].T[:piece]
 
     @pl.loop(0, height // part)
     def _(c):
@@ -489,9 +451,70 @@
         own = x0[inner, :, pl.ds(0, hd)].astype(f32)
         deltas(g0[here], z0[here], q0[here], own, dq0, dzr0, inner)
 
+    total_rows = g_ref.shape[1]
+    used = 3 * taps * piece
+    if used < total_rows:
+        for section in range(2):
+            g_ref[section, pl.ds(used, total_rows - used)] = jnp.zeros((total_rows - used, hd), f32)
+
+    depth = len(steps)
+    spans = [(0, total_rows)]
+    for k in range(depth):
+        first, length = spans[-1]
+        half = length // 2
+        spans.append((pl.multiple_of(first + bits[k] * half, 16), half))
+
+    def sum_copy(section, k):
+        if k < depth:
+            first, length = spans[k]
+            half = length // 2
+            away = pl.multiple_of(first + (1 - bits[k]) * half, 16)
+            src = sbuf.at[section, pl.ds(away, half)]
+            dst = rbuf.at[section, pl.ds(total_rows - length, half)]
+            step = k
+        else:
+            step = 2 * depth - 1 - k
+            first, length = spans[step + 1]
+            src = dst = sum_ref.at[section, pl.ds(first, length)]
+        return pltpu.make_async_remote_copy(
+            src_ref=src,
+            dst_ref=dst,
+            send_sem=sum_send.at[section, k],
+            recv_sem=sum_recv.at[section, k],
+            device_id=partners[step],
+            device_id_type=MESH,
+        )
+
+    def begin(section, k):
+        if k < depth:
+            first, length = spans[k]
+            half = length // 2
+            away = pl.multiple_of(first + (1 - bits[k]) * half, 16)
+            sbuf[section, pl.ds(away, half)] = g_ref[section, pl.ds(away, half)].astype(bf16)
+        sum_copy(section, k).start()
+
+    def finish(section, k):
+        sum_copy(section, k).wait()
+        if k < depth:
+            keep, half = spans[k + 1]
+            here = pl.ds(keep, half)
+            landed = rbuf[section, pl.ds(total_rows - 2 * half, half)]
+            summed = g_ref[section, here] + landed.astype(f32)
+            if k == depth - 1:
+                sum_ref[section, here] = summed.astype(bf16)
+            else:
+                g_ref[section, here] = summed
+
+    def turn(section, k):
+        if k >= 0:
+            finish(section, k)
+        if k + 1 < 2 * depth:
+            begin(section, k + 1)
+
     send_edges(dq0, 2)
     weight_grads_zr(1, x1, dzr1, height // part)
     weight_grads_q(1, x1, rx1, dq1, height // part)
+    turn(1, -1)
     wait_edges(dq0, 2)
 
     @pl.loop(0, width // part)
@@ -499,8 +522,12 @@
         back_reset(0, x0, g0, z0, r0, dq0, dzr0, c)
 
     send_edges(dzr0, 3)
+    turn(1, 0)
     weight_grads_q(0, x0, rx0, dq0, width // part)
+    turn(1, 1)
     weight_grads_zr(0, x0, dzr0, width // part)
+    turn(0, -1)
+    turn(1, 2)
     wait_edges(dzr0, 3)
 
     @pl.loop(0, width // part)
@@ -508,16 +535,30 @@
         cols = pl.ds(pl.multiple_of(c * part, part), part)
         hidden_back_ref[:, cols] = jnp.swapaxes(back_hidden(0, r0, dzr0, c), 0, 1)
 
-    used = 2 * 3 * taps * piece
-    if used < g_ref.shape[0]:
-        g_ref[pl.ds(used, g_ref.shape[0] - used)] = jnp.zeros((g_ref.shape[0] - used, hd), f32)
-
-
-def core(left, window, table, hidden, context, weights, hidden_grad, count, piece, sum_rows):
+    for k in range(2 * depth):
+        if k + 3 < 2 * depth:
+            turn(1, k + 3)
+        turn(0, k)
+
+    for c in chunks:
+        pl.when(has_next)(lambda c=c: onward(c).wait_send())
+        pl.when(has_next & has_prev)(lambda c=c: further(c).wait_send())
+        pl.when(near_out)(lambda c=c: band_copy(None, 2, 1, c, mate).wait_send())
+        pl.when(third_out)(lambda c=c: band_copy(2, 3, 3, c, mate).wait_send())
+
+
+def core(offset, block, left, table, hidden, context, weights, hidden_grad, pairs, count, piece, sum_rows):
     height, width, hd = hidden.shape
     taps = weights.shape[2]
     bf16, f32 = jnp.bfloat16, jnp.float32
     vmem = pl.BlockSpec(memory_space=pltpu.VMEM)
+    anywhere = pl.BlockSpec(memory_space=pl.ANY)
+    steps = sum_steps(pairs, count)
+    narrow = weights.shape
+
+    def held(values):
+        return pltpu.VMEM(values.shape, values.dtype)
+
     across = (width, height, hd)
     down = (height, width, hd)
 
@@ -525,15 +566,26 @@
         return pltpu.VMEM((shape[0] + 4, shape[1], wide * hd), bf16)
 
     return pl.pallas_call(
-        functools.partial(core_kernel, count, piece),
+        functools.partial(core_kernel, count, piece, steps),
         out_shape=(
             jax.ShapeDtypeStruct(hidden.shape, bf16),
             jax.ShapeDtypeStruct(hidden.shape, f32),
-            jax.ShapeDtypeStruct((sum_rows, hd), f32),
+            jax.ShapeDtypeStruct((2, sum_rows, hd), bf16),
         ),
-        in_specs=[vmem] * 7,
+        in_specs=[pl.BlockSpec(memory_space=pltpu.SMEM)] + [anywhere] * 7,
         out_specs=(vmem,) * 3,
         scratch_shapes=[
+            pltpu.VMEM((5,) + block.shape, bf16),
+            held(left),
+            held(table),
+            held(hidden),
+            held(context),
+            held(weights),
+            held(hidden_grad),
+            pltpu.VMEM(narrow[:3] + (2 * hd, hd), bf16),
+            pltpu.VMEM((2, sum_rows, hd), f32),
+            pltpu.VMEM((2, sum_rows, hd), bf16),
+            pltpu.VMEM((2, sum_rows, hd), bf16),
             pltpu.VMEM((width, height, 4 * width), f32),
             padded(across, 2),
             padded(down, 2),
@@ -553,34 +605,23 @@
             pltpu.VMEM((taps, 2 * hd, 2 * hd), f32),
             pltpu.SemaphoreType.DMA((4, 2)),
             pltpu.SemaphoreType.DMA((4, 2)),
+            pltpu.SemaphoreType.DMA((4, BAND_CHUNKS)),
+            pltpu.SemaphoreType.DMA((4, BAND_CHUNKS)),
+            pltpu.SemaphoreType.DMA((2, 2 * len(steps))),
+            pltpu.SemaphoreType.DMA((2, 2 * len(steps))),
+            pltpu.SemaphoreType.DMA((7,)),
         ],
         compiler_params=pltpu.CompilerParams(
-            collective_id=2, has_side_effects=True, vmem_limit_bytes=58 * 1024 * 1024
+            collective_id=0, has_side_effects=True, vmem_limit_bytes=58 * 1024 * 1024
         ),
         name="core",
-    )(left, window, table, hidden, context, weights, hidden_grad)
+    )(offset, block, left, table, hidden, context, weights, hidden_grad)
 
 
 def on_device(left_feats, right_feats, offsets, hidden, context, gru_weights, hidden_grad):
     left_block = left_feats[0]
     right_block = right_feats[0]
-    offset = offsets[0]
-    stripe = lax.axis_index("blk")
     column_count = left_block.shape[1]
-    empty_block = jnp.zeros_like(right_block)
-    low_id = stripe - offset - 1
-    high_id = stripe - offset
-    band = band_exchange(right_block, lax.axis_size("blk"))
-
-    def pick_one(block_id):
-        distance = jnp.clip(stripe - block_id, 0, 4)
-        picked = lax.dynamic_index_in_dim(band, jnp.maximum(distance - 1, 0), 0, keepdims=False)
-        picked = jnp.where(distance == 0, right_block, picked)
-        return jnp.where(block_id >= 0, picked, empty_block)
-
-    low_block = pick_one(low_id)
-    high_block = pick_one(high_id)
-    window = jnp.concatenate([low_block, high_block], axis=1)
     table = lookup_table(column_count, LEVELS, RADIUS) / math.sqrt(left_block.shape[-1])
     hd = gru_weights.shape[-1]
     table = np.concatenate([table, table], axis=1)
@@ -589,21 +630,22 @@
     pairs, blks = lax.axis_size("pair"), lax.axis_size("blk")
     shape = gru_weights.shape
     piece = -(-shape[3] // 8) * 8
-    used = math.prod(shape[:3]) * piece
-    weights = jnp.pad(gru_weights, ((0, 0),) * 3 + ((0, 2 * hd - shape[3]), (0, 0)))
-    new_hidden, hidden_back, rows = core(
+    used = math.prod(shape[1:3]) * piece
+    new_hidden, hidden_back, summed = core(
+        offsets,
+        right_block,
         left_block,
-        window,
         table,
         hidden[0],
         context[0],
-        weights,
+        gru_weights,
         hidden_grad[0],
+        pairs,
         blks,
         piece,
         sum_rows_count(used, pairs * blks),
     )
-    summed = all_sum(rows, pairs, blks)[:used].reshape(shape[:3] + (piece, hd))
+    summed = summed[:, :used].reshape(shape[:3] + (piece, hd))
     grad_stack = summed[:, :, :, : shape[3]].astype(jnp.float32)
     return (new_hidden[None], grad_stack, hidden_back[None])
 

time: 158 us -> 141 us (0.89)
  Pallas kernels: 145 us -> 131 us
  other arithmetic: 5.66 us -> 2.43 us
    pallas_call x3 -> x1, Pallas kernels: 145 us -> 131 us  [core(): pl.pallas_call(functools.partial(core_kernel, count, piece, steps), out_s...]
    select_n x1 -> x0, other arithmetic: 1.73 us -> none  [pick_one(): return jnp.where(block_id >= 0, picked, empty_block)]
    unnamed x13 -> x7, local copies, waits for them, and re-layouts: 3.87 us -> 4.91 us
where the time goes in v1:
time: 141 us
  Pallas kernels  131 us (93%)
  local copies, waits for them, and re-layouts  6.3 us (4%)
  other arithmetic  2.43 us (2%)
    pallas_call x1, Pallas kernels, core(): pl.pallas_call(functools.partial(core_kernel, count, piece, steps), out_s...  131 us
    unnamed x7, local copies, waits for them, and re-layouts  4.91 us

profile of v1, /device:TPU:0, one launch (start us, length us, event | category | flops | bytes accessed | tf_op | source)
XLA Modules:
  0.0 140.8 jit_solution(2023320173478872586)
XLA Ops:
  1.3 2.5 %copy.11.weights_in = bf16[2,3,5,164,128]{4,3,2,1,0:T(8,128)(2,1)} copy(bf16[2,3,5,164,128]{4,0,3,2,1:T(2,128)(2,1)} %param.13) | data formatting | bytes 2519040 | tf_op args[5]
  3.8 130.8 %core.1 = (bf16[64,32,128]{2,1,0:T(8,128)(2,1)}, f32[64,32,128]{2,1,0:T(8,128)}, bf16[2,2560,128]{2,1,0:T(8,128)(2,1)}) custom-call(s32[1]{0:T(128)S(6)} %copy.17.offset_ref, bf16[64,32,256]{2,1,0:T(8,128)(2,1)} %bitcast.12, bf16[64,32,256]{2,1,0:T(8,128)(2,1)} %bitcast.13, bf16[32,128,128]{2,1,0:T(8,128)(2,1)} %constant.2.clone.table_in, ...), custom_call_target="tpu_custom_call" | custom-call | tf_op jit(solution)/shard_map/core/pallas_call | solution.py:568
  134.6 1.4 slice.6
  136.0 0.0 copy-start.1
  136.0 2.4 %copy_convert_fusion = f32[2,3,5,164,128]{4,0,3,2,1:T(2,128)} fusion(bf16[2,3,5,164,128]{4,3,2,1,0:T(8,128)(2,1)S(1)} %bitcast.9), kind=kLoop, calls=%fused_computation | loop fusion | flops 629760 | bytes 3778560 | tf_op jit(solution)/shard_map/convert_element_type | solution.py:649
  138.4 0.0 copy-done.1
  138.4 0.0 copy-start
  138.4 0.8 copy.18
  139.2 0.6 copy-done
  139.8 1.0 copy.19
Async XLA Ops:
  136.0 2.4 %copy-start.1 = (bf16[64,32,128]{2,1,0:T(8,128)(2,1)S(1)}, bf16[64,32,128]{2,1,0:T(8,128)(2,1)}, u32[]{:S(2)}) copy-start(bf16[64,32,128]{2,1,0:T(8,128)(2,1)} %get-tuple-element.6) | copy-start | bytes 1572868
  138.4 1.4 %copy-start = (f32[64,32,128]{2,1,0:T(8,128)S(1)}, f32[64,32,128]{2,1,0:T(8,128)}, u32[]{:S(2)}) copy-start(f32[64,32,128]{2,1,0:T(8,128)} %get-tuple-element.8) | copy-start | bytes 3145732

commit v2 on v1

--- a/solution.py
+++ b/solution.py
@@ -40,11 +40,12 @@
 
 def sum_steps(pairs, blks):
     steps = []
-    for axis, size in (("pair", pairs), ("blk", blks)):
-        mask = 1
-        while mask < size:
-            steps.append((axis, mask))
-            mask *= 2
+    for axis, size, most in (("pair", pairs, 2), ("blk", blks, 8)):
+        stride = 1
+        while stride < size:
+            members = min(most, size // stride)
+            steps.append((axis, stride, members))
+            stride *= members
     return steps
 
 
@@ -132,17 +133,27 @@
 
     barrier = pltpu.get_barrier_semaphore()
     places = {"pair": lax.axis_index("pair"), "blk": me}
-    bits = []
+    ranks = []
     partners = []
-    for axis, mask in steps:
-        bit = lax.rem(places[axis] // mask, 2)
-        bits.append(bit)
-        partners.append({axis: places[axis] + mask * (1 - 2 * bit)})
-        pl.semaphore_signal(barrier, inc=1, device_id=partners[-1], device_id_type=MESH)
+    for axis, stride, members in steps:
+        place = places[axis]
+        ranks.append(lax.rem(place // stride, members))
+        row = [None]
+        for d in range(1, members):
+            shift = 0
+            mask = 1
+            while mask < members:
+                if d & mask:
+                    bit = lax.rem(place // (stride * mask), 2)
+                    shift = shift + stride * mask * (1 - 2 * bit)
+                mask *= 2
+            row.append((place + shift, axis))
+            pl.semaphore_signal(barrier, inc=1, device_id={axis: place + shift}, device_id_type=MESH)
+        partners.append(row)
     has_next = me + 2 < count
     has_prev = me >= 2
     has_far = me >= 4
-    expected = len(steps)
+    expected = sum(members - 1 for _, _, members in steps)
     for present, shift in ((has_left, -1), (has_right, 1), (has_prev, -2), (has_next, 2)):
 
         @pl.when(present)
@@ -264,31 +275,33 @@
                     [rest, blank], axis=0
                 ).astype(bf16)
 
-    for c in chunks:
-
-        @pl.when(has_far)
-        def _(c=c):
-            further(c).wait_recv()
-            pl.when(odd == 1)(lambda: band_copy(4, 3, 3, c, mate).start())
-
     near_in = (odd == 1) | has_prev
     third_in = ((odd == 1) & has_prev) | ((odd == 0) & has_far)
     near_out = (odd == 0) | has_prev
     third_out = ((odd == 0) & has_prev) | ((odd == 1) & has_far)
-    for c in chunks:
-        pl.when(near_in)(lambda c=c: band_copy(None, 2, 1, c, mate).wait_recv())
-        pl.when(third_in)(lambda c=c: band_copy(2, 3, 3, c, mate).wait_recv())
-
     offset = offset_ref[0]
-
-    @pl.loop(0, height // part)
-    def _(c):
-        rows = pl.ds(pl.multiple_of(c * part, part), part)
-        window = jnp.concatenate([band[offset + 1, rows], band[offset, rows]], axis=1)
-        scores = jnp.einsum("hxc,hjc->hxj", left_ref[rows], window, preferred_element_type=f32)
-        scores = jnp.swapaxes(scores, 0, 1)
-        high = scores.astype(bf16).astype(f32)
-        corr[:, rows] = jnp.concatenate([high, scores - high], axis=-1)
+    for c in range(BAND_CHUNKS + 1):
+        if c < BAND_CHUNKS:
+
+            @pl.when(has_far)
+            def _(c=c):
+                further(c).wait_recv()
+                pl.when(odd == 1)(lambda: band_copy(4, 3, 3, c, mate).start())
+
+        if c >= 1:
+            pl.when(near_in)(lambda c=c: band_copy(None, 2, 1, c - 1, mate).wait_recv())
+            pl.when(third_in)(lambda c=c: band_copy(2, 3, 3, c - 1, mate).wait_recv())
+            rows = pl.ds((c - 1) * band_rows, band_rows)
+            slots = [band[slot, rows] for slot in range(5)]
+            low, high = slots[1], slots[0]
+            for shift in range(1, 4):
+                low = jnp.where(offset == shift, slots[shift + 1], low)
+                high = jnp.where(offset == shift, slots[shift], high)
+            window = jnp.concatenate([low, high], axis=1)
+            scores = jnp.einsum("hxc,hjc->hxj", left_ref[rows], window, preferred_element_type=f32)
+            scores = jnp.swapaxes(scores, 0, 1)
+            high = scores.astype(bf16).astype(f32)
+            corr[:, rows] = jnp.concatenate([high, scores - high], axis=-1)
 
     @pl.loop(0, width // part)
     def _(c):
@@ -461,45 +474,60 @@
     spans = [(0, total_rows)]
     for k in range(depth):
         first, length = spans[-1]
-        half = length // 2
-        spans.append((pl.multiple_of(first + bits[k] * half, 16), half))
-
-    def sum_copy(section, k):
+        share = length // steps[k][2]
+        spans.append((pl.multiple_of(first + ranks[k] * share, 16), share))
+    landing = [0]
+    for k in range(depth):
+        landing.append(landing[-1] + spans[k][1] - spans[k + 1][1])
+
+    def away(step, d):
+        axis, stride, members = steps[step]
+        target = lax.rem(partners[step][d][0] // stride, members)
+        first, _ = spans[step]
+        share = spans[step + 1][1]
+        return pl.ds(pl.multiple_of(first + target * share, 16), share)
+
+    def sum_copies(section, k):
+        step = k if k < depth else 2 * depth - 1 - k
+        copies = []
+        for d in range(1, steps[step][2]):
+            share = spans[step + 1][1]
+            if k < depth:
+                src = sbuf.at[section, away(step, d)]
+                dst = rbuf.at[section, pl.ds(landing[step] + (d - 1) * share, share)]
+            else:
+                src = dst = sum_ref.at[section, pl.ds(spans[step + 1][0], share)]
+            place, axis = partners[step][d]
+            copies.append(
+                pltpu.make_async_remote_copy(
+                    src_ref=src,
+                    dst_ref=dst,
+                    send_sem=sum_send.at[section, k, d],
+                    recv_sem=sum_recv.at[section, k, d],
+                    device_id={axis: place},
+                    device_id_type=MESH,
+                )
+            )
+        return copies
+
+    def begin(section, k):
+        copies = sum_copies(section, k)
+        for d in range(1, len(copies) + 1):
+            if k < depth:
+                there = away(k, d)
+                sbuf[section, there] = g_ref[section, there].astype(bf16)
+            copies[d - 1].start()
+
+    def finish(section, k):
+        for copy in sum_copies(section, k):
+            copy.wait()
         if k < depth:
-            first, length = spans[k]
-            half = length // 2
-            away = pl.multiple_of(first + (1 - bits[k]) * half, 16)
-            src = sbuf.at[section, pl.ds(away, half)]
-            dst = rbuf.at[section, pl.ds(total_rows - length, half)]
-            step = k
-        else:
-            step = 2 * depth - 1 - k
-            first, length = spans[step + 1]
-            src = dst = sum_ref.at[section, pl.ds(first, length)]
-        return pltpu.make_async_remote_copy(
-            src_ref=src,
-            dst_ref=dst,
-            send_sem=sum_send.at[section, k],
-            recv_sem=sum_recv.at[section, k],
-            device_id=partners[step],
-            device_id_type=MESH,
-        )
-
-    def begin(section, k):
-        if k < depth:
-            first, length = spans[k]
-            half = length // 2
-            away = pl.multiple_of(first + (1 - bits[k]) * half, 16)
-            sbuf[section, pl.ds(away, half)] = g_ref[section, pl.ds(away, half)].astype(bf16)
-        sum_copy(section, k).start()
-
-    def finish(section, k):
-        sum_copy(section, k).wait()
-        if k < depth:
-            keep, half = spans[k + 1]
-            here = pl.ds(keep, half)
-            landed = rbuf[section, pl.ds(total_rows - 2 * half, half)]
-            summed = g_ref[section, here] + landed.astype(f32)
+            keep, share = spans[k + 1]
+            here = pl.ds(keep, share)
+            summed = g_ref[section, here]
+            for d in range(1, steps[k][2]):
+                landed = rbuf[section, pl.ds(landing[k] + (d - 1) * share, share)]
+                summed = summed + landed.astype(f32)
             if k == depth - 1:
                 sum_ref[section, here] = summed.astype(bf16)
             else:
@@ -607,8 +635,8 @@
             pltpu.SemaphoreType.DMA((4, 2)),
             pltpu.SemaphoreType.DMA((4, BAND_CHUNKS)),
             pltpu.SemaphoreType.DMA((4, BAND_CHUNKS)),
-            pltpu.SemaphoreType.DMA((2, 2 * len(steps))),
-            pltpu.SemaphoreType.DMA((2, 2 * len(steps))),
+            pltpu.SemaphoreType.DMA((2, 2 * len(steps), 8)),
+            pltpu.SemaphoreType.DMA((2, 2 * len(steps), 8)),
             pltpu.SemaphoreType.DMA((7,)),
         ],
         compiler_params=pltpu.CompilerParams(

time: 141 us -> 140 us (level)
  Pallas kernels: 131 us -> 129 us
where the time goes in v2:
time: 140 us; the launch traced here: 139 us
  Pallas kernels  129 us (92%)
  local copies, waits for them, and re-layouts  6.3 us (4%)
  other arithmetic  2.43 us (2%)
    pallas_call x1, Pallas kernels, core(): pl.pallas_call(functools.partial(core_kernel, count, piece, steps), out_s...  129 us
    unnamed x7, local copies, waits for them, and re-layouts  4.91 us

profile of v2, /device:TPU:0, one launch (start us, length us, event | category | flops | bytes accessed | tf_op | source)
XLA Modules:
  0.0 139.4 jit_solution(2105992808828626716)
XLA Ops:
  1.3 2.5 %copy.11.weights_in = bf16[2,3,5,164,128]{4,3,2,1,0:T(8,128)(2,1)} copy(bf16[2,3,5,164,128]{4,0,3,2,1:T(2,128)(2,1)} %param.13) | data formatting | bytes 2519040 | tf_op args[5]
  3.8 129.4 %core.1 = (bf16[64,32,128]{2,1,0:T(8,128)(2,1)}, f32[64,32,128]{2,1,0:T(8,128)}, bf16[2,2560,128]{2,1,0:T(8,128)(2,1)}) custom-call(s32[1]{0:T(128)S(6)} %copy.17.offset_ref, bf16[64,32,256]{2,1,0:T(8,128)(2,1)} %bitcast.12, bf16[64,32,256]{2,1,0:T(8,128)(2,1)} %bitcast.13, bf16[32,128,128]{2,1,0:T(8,128)(2,1)} %constant.2.clone.table_in, ...), custom_call_target="tpu_custom_call" | custom-call | tf_op jit(solution)/shard_map/core/pallas_call | solution.py:596
  133.2 1.4 %slice.6 = bf16[2,2520,128]{2,1,0:T(8,128)(2,1)S(1)} slice(bf16[2,2560,128]{2,1,0:T(8,128)(2,1)} %get-tuple-element.7), slice={[0:2], [0:2520], [0:128]} | slice | bytes 2580480 | tf_op jit(solution)/shard_map/slice | solution.py:676
  134.6 0.0 copy-start.1
  134.6 2.4 %copy_convert_fusion = f32[2,3,5,164,128]{4,0,3,2,1:T(2,128)} fusion(bf16[2,3,5,164,128]{4,3,2,1,0:T(8,128)(2,1)S(1)} %bitcast.9), kind=kLoop, calls=%fused_computation | loop fusion | flops 629760 | bytes 3778560 | tf_op jit(solution)/shard_map/convert_element_type | solution.py:677
  137.1 0.0 copy-done.1
  137.1 0.0 copy-start
  137.1 0.8 copy.18
  137.9 0.6 copy-done
  138.5 1.0 copy.19
Async XLA Ops:
  134.6 2.4 %copy-start.1 = (bf16[64,32,128]{2,1,0:T(8,128)(2,1)S(1)}, bf16[64,32,128]{2,1,0:T(8,128)(2,1)}, u32[]{:S(2)}) copy-start(bf16[64,32,128]{2,1,0:T(8,128)(2,1)} %get-tuple-element.6) | copy-start | bytes 1572868
  137.1 1.4 %copy-start = (f32[64,32,128]{2,1,0:T(8,128)S(1)}, f32[64,32,128]{2,1,0:T(8,128)}, u32[]{:S(2)}) copy-start(f32[64,32,128]{2,1,0:T(8,128)} %get-tuple-element.8) | copy-start | bytes 3145732

commit v3 on v2

--- a/solution.py
+++ b/solution.py
@@ -471,33 +471,39 @@
             g_ref[section, pl.ds(used, total_rows - used)] = jnp.zeros((total_rows - used, hd), f32)
 
     depth = len(steps)
-    spans = [(0, total_rows)]
-    for k in range(depth):
-        first, length = spans[-1]
-        share = length // steps[k][2]
-        spans.append((pl.multiple_of(first + ranks[k] * share, 16), share))
-    landing = [0]
-    for k in range(depth):
-        landing.append(landing[-1] + spans[k][1] - spans[k + 1][1])
-
-    def away(step, d):
-        axis, stride, members = steps[step]
-        target = lax.rem(partners[step][d][0] // stride, members)
-        first, _ = spans[step]
-        share = spans[step + 1][1]
-        return pl.ds(pl.multiple_of(first + target * share, 16), share)
+    orders = ([0, *range(2, depth), 1], list(range(depth)))
+    spans = []
+    landing = []
+    for order in orders:
+        row = [(0, total_rows)]
+        places_in = [0]
+        for at in order:
+            first, length = row[-1]
+            share = length // steps[at][2]
+            row.append((pl.multiple_of(first + ranks[at] * share, 16), share))
+            places_in.append(places_in[-1] + length - share)
+        spans.append(row)
+        landing.append(places_in)
+
+    def away(section, k, d):
+        at = orders[section][k]
+        axis, stride, members = steps[at]
+        target = lax.rem(partners[at][d][0] // stride, members)
+        share = spans[section][k + 1][1]
+        return pl.ds(pl.multiple_of(spans[section][k][0] + target * share, 16), share)
 
     def sum_copies(section, k):
         step = k if k < depth else 2 * depth - 1 - k
+        at = orders[section][step]
+        own, share = spans[section][step + 1]
         copies = []
-        for d in range(1, steps[step][2]):
-            share = spans[step + 1][1]
+        for d in range(1, steps[at][2]):
             if k < depth:
-                src = sbuf.at[section, away(step, d)]
-                dst = rbuf.at[section, pl.ds(landing[step] + (d - 1) * share, share)]
+                src = sbuf.at[section, away(section, step, d)]
+                dst = rbuf.at[section, pl.ds(landing[section][step] + (d - 1) * share, share)]
             else:
-                src = dst = sum_ref.at[section, pl.ds(spans[step + 1][0], share)]
-            place, axis = partners[step][d]
+                src = dst = sum_ref.at[section, pl.ds(own, share)]
+            place, axis = partners[at][d]
             copies.append(
                 pltpu.make_async_remote_copy(
                     src_ref=src,
@@ -514,7 +520,7 @@
         copies = sum_copies(section, k)
         for d in range(1, len(copies) + 1):
             if k < depth:
-                there = away(k, d)
+                there = away(section, k, d)
                 sbuf[section, there] = g_ref[section, there].astype(bf16)
             copies[d - 1].start()
 
@@ -522,11 +528,11 @@
         for copy in sum_copies(section, k):
             copy.wait()
         if k < depth:
-            keep, share = spans[k + 1]
+            keep, share = spans[section][k + 1]
             here = pl.ds(keep, share)
             summed = g_ref[section, here]
-            for d in range(1, steps[k][2]):
-                landed = rbuf[section, pl.ds(landing[k] + (d - 1) * share, share)]
+            for d in range(1, steps[orders[section][k]][2]):
+                landed = rbuf[section, pl.ds(landing[section][k] + (d - 1) * share, share)]
                 summed = summed + landed.astype(f32)
             if k == depth - 1:
                 sum_ref[section, here] = summed.astype(bf16)

time: 140 us -> 137 us (0.979)
  Pallas kernels: 129 us -> 127 us
    pallas_call x1, Pallas kernels: 129 us -> 127 us  [core(): pl.pallas_call(functools.partial(core_kernel, count, piece, steps), out_s...]
where the time goes in v3:
time: 137 us
  Pallas kernels  127 us (93%)
  local copies, waits for them, and re-layouts  6.3 us (5%)
  other arithmetic  2.43 us (2%)
    pallas_call x1, Pallas kernels, core(): pl.pallas_call(functools.partial(core_kernel, count, piece, steps), out_s...  127 us
    unnamed x7, local copies, waits for them, and re-layouts  4.91 us

profile of v3, /device:TPU:0, one launch (start us, length us, event | category | flops | bytes accessed | tf_op | source)
XLA Modules:
  0.0 136.7 jit_solution(17003796610564195102)
XLA Ops:
  1.3 2.5 %copy.11.weights_in = bf16[2,3,5,164,128]{4,3,2,1,0:T(8,128)(2,1)} copy(bf16[2,3,5,164,128]{4,0,3,2,1:T(2,128)(2,1)} %param.13) | data formatting | bytes 2519040 | tf_op args[5]
  3.8 126.7 %core.1 = (bf16[64,32,128]{2,1,0:T(8,128)(2,1)}, f32[64,32,128]{2,1,0:T(8,128)}, bf16[2,2560,128]{2,1,0:T(8,128)(2,1)}) custom-call(s32[1]{0:T(128)S(6)} %copy.17.offset_ref, bf16[64,32,256]{2,1,0:T(8,128)(2,1)} %bitcast.12, bf16[64,32,256]{2,1,0:T(8,128)(2,1)} %bitcast.13, bf16[32,128,128]{2,1,0:T(8,128)(2,1)} %constant.2.clone.table_in, ...), custom_call_target="tpu_custom_call" | custom-call | tf_op jit(solution)/shard_map/core/pallas_call | solution.py:602
  130.5 1.4 %slice.6 = bf16[2,2520,128]{2,1,0:T(8,128)(2,1)S(1)} slice(bf16[2,2560,128]{2,1,0:T(8,128)(2,1)} %get-tuple-element.7), slice={[0:2], [0:2520], [0:128]} | slice | bytes 2580480 | tf_op jit(solution)/shard_map/slice | solution.py:682
  131.9 0.0 copy-start.1
  131.9 2.4 %copy_convert_fusion = f32[2,3,5,164,128]{4,0,3,2,1:T(2,128)} fusion(bf16[2,3,5,164,128]{4,3,2,1,0:T(8,128)(2,1)S(1)} %bitcast.9), kind=kLoop, calls=%fused_computation | loop fusion | flops 629760 | bytes 3778560 | tf_op jit(solution)/shard_map/convert_element_type | solution.py:683
  134.3 0.0 copy-done.1
  134.3 0.0 copy-start
  134.3 0.8 copy.18
  135.1 0.6 copy-done
  135.7 1.0 copy.19
Async XLA Ops:
  131.9 2.4 %copy-start.1 = (bf16[64,32,128]{2,1,0:T(8,128)(2,1)S(1)}, bf16[64,32,128]{2,1,0:T(8,128)(2,1)}, u32[]{:S(2)}) copy-start(bf16[64,32,128]{2,1,0:T(8,128)(2,1)} %get-tuple-element.6) | copy-start | bytes 1572868
  134.3 1.4 %copy-start = (f32[64,32,128]{2,1,0:T(8,128)S(1)}, f32[64,32,128]{2,1,0:T(8,128)}, u32[]{:S(2)}) copy-start(f32[64,32,128]{2,1,0:T(8,128)} %get-tuple-element.8) | copy-start | bytes 3145732
